TPU v7x, 256 devices: a whole 4x4x8 slice. The times are simulated.
256 devices in a mesh: dp: 16 (over x_lo, y, core), tensor: 16 (over z, x_hi).
Axes of the slice: x: 4 (x_hi: 2, x_lo: 2; x = x_hi * 2 + x_lo), y: 4, z: 8, core: 2. Of those that a mesh axis runs over, the one named last changes fastest.
Arguments:
- target_hidden: bfloat16 [512, 16384], P('dp', 'tensor'), may hold values from -64 to 64
- target_gain: bfloat16 [16384], replicated, may hold values from 0.25 to 1.75
- target_head: bfloat16 [16384, 65536], P(None, ('dp', 'tensor')), may hold values from -8 to 8
- reference_hidden: bfloat16 [512, 4096], P('dp', 'tensor'), may hold values from -64 to 64
- reference_gain: bfloat16 [4096], replicated, may hold values from 0.25 to 1.75
- reference_head: bfloat16 [4096, 65536], P(None, ('dp', 'tensor')), may hold values from -8 to 8
Outputs:
- contrast: float32 [512, 65536], P(None, ('dp', 'tensor'))
All inputs are finite; a program needn't handle non-finite values.
Results may differ from a plain program's by a relative error of at most 0.0012.
Values may be sent and summed in bfloat16 or wider, within the bound.
No kernel may reach another device: no remote copies, remote signals or barrier semaphores. Data moves between devices by JAX's collectives and lax.ppermute only.
A program may use at most 128 MiB of HBM per device.

v0:
```python
import jax
import jax.numpy as jnp
from jax import lax
from jax.sharding import PartitionSpec as P

EPS = 1e-05
LOG_TEN = 2.302585092994046


def normalize_full(piece, gain):
    values = piece.astype(jnp.float32)
    square_mean = jnp.mean(values * values, axis=1, keepdims=True)
    return (values * lax.rsqrt(square_mean + EPS) * gain.astype(jnp.float32)).astype(jnp.bfloat16)


def local(
    target_hidden, target_gain, target_head, reference_hidden, reference_gain, reference_head
):
    wide_t, wide_r = (
        lax.all_gather(target_hidden, "tensor", axis=1, tiled=True),
        lax.all_gather(reference_hidden, "tensor", axis=1, tiled=True),
    )
    logits_t = jnp.dot(
        normalize_full(lax.all_gather(wide_t, "dp", axis=0, tiled=True), target_gain),
        target_head,
        preferred_element_type=jnp.float32,
    )
    logits_r = jnp.dot(
        normalize_full(lax.all_gather(wide_r, "dp", axis=0, tiled=True), reference_gain),
        reference_head,
        preferred_element_type=jnp.float32,
    )
    local_peak_t = jnp.max(logits_t, axis=1)
    local_peak_r = jnp.max(logits_r, axis=1)
    peak_t, peak_r = lax.pmax((local_peak_t, local_peak_r), ("dp", "tensor"))
    local_total_t = jnp.sum(jnp.exp(logits_t - peak_t[:, None]), axis=1)
    local_total_r = jnp.sum(jnp.exp(logits_r - peak_r[:, None]), axis=1)
    total_t, total_r = lax.psum((local_total_t, local_total_r), ("dp", "tensor"))
    lse_t = (peak_t + jnp.log(total_t))[:, None]
    lse_r = (peak_r + jnp.log(total_r))[:, None]
    margin = jnp.minimum(0.0, logits_t - peak_t[:, None] + LOG_TEN)
    return logits_t - lse_t - 0.5 * (logits_r - lse_r) + margin


def solution(mesh):
    placed = (
        P("dp", "tensor"),
        P(),
        P(None, ("dp", "tensor")),
        P("dp", "tensor"),
        P(),
        P(None, ("dp", "tensor")),
    )
    return jax.shard_map(
        local, mesh=mesh, in_specs=placed, out_specs=P(None, ("dp", "tensor")), check_vma=False
    )
```

profile of v0, /device:TPU:1, one launch (start us, length us, event | category | flops | bytes accessed | tf_op | source)
XLA Modules:
  0.0 408.6 jit_solution(10341636960921009847)
XLA Ops:
  6.5 0.0 copy-start
  6.5 0.0 all-gather.4.cloned.1.call-start
  6.5 0.7 all-gather.4.cloned.1.call-update
  7.3 0.0 all-gather.8.cloned.1.call-start
  7.3 42.1 %all_gather.14 = bf16[32,4096]{1,0:T(8,128)(2,1)} all-gather(bf16[32,256]{1,0:T(8,128)(2,1)} %param.9), channel_id=1, replica_groups=mesh['dp'=16,'tensor'=16] {'tensor'}, dimensions={1}, use_global_device_ids=true | all-gather | bytes 278528 | tf_op jit(solution)/shard_map/all_gather | solution.py:21
  49.4 0.0 all-gather.8.cloned.1.call-update
  49.5 0.0 all-gather.6.cloned.1.call-start
  49.5 39.4 %all-gather.4.cloned.1.call-done = bf16[32,16384]{1,0:T(8,128)(2,1)} async-done(((bf16[32,1024]{1,0:T(8,128)(2,1)}), bf16[32,16384]{1,0:T(8,128)(2,1)}) %all-gather.4.cloned.1.call-update) | async-done | bytes 1048592 | tf_op jit(solution)/shard_map/all_gather | solution.py:20
  88.9 0.0 all-gather.6.cloned.1.call-update
  88.9 0.7 convert_element_type.22
  89.6 0.8 convert_element_type.19
  90.4 41.0 %all-gather.8.cloned.1.call-done = bf16[512,4096]{1,0:T(8,128)(2,1)} async-done(((bf16[32,4096]{1,0:T(8,128)(2,1)}), bf16[512,4096]{1,0:T(8,128)(2,1)}) %all-gather.8.cloned.1.call-update) | async-done | bytes 4194320 | tf_op jit(solution)/shard_map/all_gather | solution.py:29
  131.4 3.1 fusion.7
  134.5 0.0 copy-done
  134.5 3.8 fusion.14
  138.3 89.3 %all-gather.6.cloned.1.call-done = bf16[512,16384]{1,0:T(8,128)(2,1)} async-done(((bf16[32,16384]{1,0:T(8,128)(2,1)}), bf16[512,16384]{1,0:T(8,128)(2,1)}) %all-gather.6.cloned.1.call-update) | async-done | bytes 16777232 | tf_op jit(solution)/shard_map/all_gather | solution.py:24
  227.5 7.2 %fusion = f32[512]{0:T(512)S(1)} fusion(bf16[512,16384]{1,0:T(8,128)(2,1)} %all-gather.6.cloned.1.call-done), kind=kLoop, calls=%fused_computation.2 | loop fusion | flops 25165312 | bytes 16779264 | tf_op jit(solution)/shard_map/reduce_sum | solution.py:12
  234.7 13.6 %fusion.15 = (f32[512]{0:T(512)S(1)}, f32[512,256]{0,1:T(8,128)S(1)}) fusion(bf16[16384,256]{1,0:T(8,128)(2,1)} %param.8, bf16[512,16384]{1,0:T(8,128)(2,1)} %all-gather.6.cloned.1.call-done, f32[16384]{0:T(1024)S(1)} %convert_element_type.19, f32[512]{0:T(512)S(1)} %add_rsqrt_fusion.1), kind=kOutput, calls=%fused_computation.24 | convolution fusion | flops 4328652288 | bytes 25759744 | tf_op jit(solution)/shard_map/dot_general | solution.py:23
  248.4 77.0 %all-reduce.1 = (f32[512]{0:T(512)S(1)}, f32[512]{0:T(512)S(1)}) all-reduce(f32[512]{0:T(512)S(1)} %get-tuple-element.9, f32[512]{0:T(512)S(1)} %get-tuple-element.11), channel_id=1, replica_groups=mesh['dp'=16,'tensor'=16] {'dp','tensor'}, use_global_device_ids=true, to_apply=%region_7.0 | all-reduce | flops 1024 | bytes 8192 | tf_op jit(solution)/shard_map/pmax | solution.py:35
  325.4 0.2 exponential_reduce_fusion
  325.6 73.6 %all-reduce = (f32[512]{0:T(512)S(1)}, f32[512]{0:T(512)S(1)}) all-reduce(f32[512]{0:T(512)S(1)} %get-tuple-element.13, f32[512]{0:T(512)S(1)} %get-tuple-element.14), channel_id=1, replica_groups=mesh['dp'=16,'tensor'=16] {'dp','tensor'}, use_global_device_ids=true, to_apply=%region_9.0 | all-reduce | flops 1024 | bytes 8192 | tf_op jit(solution)/shard_map/psum | solution.py:38
  399.1 0.9 minimum_add_fusion
  400.1 2.0 copy.7
  (4 shorter events, 0.0 us)
Async XLA Ops:
  6.5 128.0 %copy-start = (bf16[4096,256]{1,0:T(8,128)(2,1)S(1)}, bf16[4096,256]{1,0:T(8,128)(2,1)}, u32[]{:S(2)}) copy-start(bf16[4096,256]{1,0:T(8,128)(2,1)} %param.11) | copy-start | bytes 6291460
  6.5 82.4 %all-gather.4.cloned.1.call-start = ((), (), s32[]{:S(2)}) async-start(), calls=%async_computation | async-start | bytes 1114112 | tf_op jit(solution)/shard_map/all_gather | solution.py:20
  7.3 124.1 %all-gather.8.cloned.1.call-start = ((), (), s32[]{:S(2)}) async-start(), calls=%async_computation.2 | async-start | bytes 4456448 | tf_op jit(solution)/shard_map/all_gather | solution.py:29
  49.5 178.1 %all-gather.6.cloned.1.call-start = ((), (), s32[]{:S(2)}) async-start(), calls=%async_computation.1 | async-start | bytes 17825792 | tf_op jit(solution)/shard_map/all_gather | solution.py:24
Sparse Core Ops, SparseCore 0:
  10.0 78.8 all-gather.3
  90.7 40.6 all-gather.7
  133.3 94.2 all-gather.5
where the time goes:
time: 409 us
  blocking collectives  193 us (47%)
  waiting for transfers between devices  170 us (42%)
  matrix products  17.4 us (4%)
  between operations  13.1 us (3%)
  other arithmetic  12.9 us (3%)
    all_gather x1, waiting for transfers between devices, local(): lax.all_gather(wide_t, 'dp', axis=0, tiled=True)  89.3 us
    pmax x1, blocking collectives, local(): peak_t, peak_r = lax.pmax((local_peak_t, local_peak_r), ('dp', 'tensor'))  77 us
    psum x1, blocking collectives, local(): lax.psum((local_total_t, local_total_r), ('dp', 'tensor'))  73.6 us
    all_gather x1, blocking collectives, local(): lax.all_gather(reference_hidden, 'tensor', axis=1, tiled=True)  42.1 us
    all_gather x1, waiting for transfers between devices, local(): lax.all_gather(wide_r, 'dp', axis=0, tiled=True)  41 us
    all_gather x1, waiting for transfers between devices, local(): lax.all_gather(target_hidden, 'tensor', axis=1, tiled=True)  39.4 us
    dot_general x1, matrix products, local(): jnp.dot(normalize_full(lax.all_gather(wide_t, 'dp', axis=0, tiled=True),...  13.6 us
    reduce_sum x2, other arithmetic, normalize_full(): square_mean = jnp.mean(values * values, axis=1, keepdims=True)  10.3 us
  transfers between devices with their start and end apart: 3, of which 3 were waited for; matrix products, arithmetic and copies ran while one was open for 2% of the time, Pallas kernels for 0%

commit v1 on v0

--- a/solution.py
+++ b/solution.py
@@ -5,6 +5,13 @@
 
 EPS = 1e-05
 LOG_TEN = 2.302585092994046
+
+
+def push_rounds(sheet, device_axis, d0=1):
+    d_next = lax.axis_size(device_axis)
+    val2 = jnp.stack(d_next * [sheet], axis=0)
+    front = lax.all_to_all(val2, split_axis=0, concat_axis=0, axis_name=device_axis)
+    return jnp.concatenate(front, d0)
 
 
 def normalize_full(piece, gain):
@@ -18,7 +25,7 @@
 ):
     wide_t, wide_r = (
         lax.all_gather(target_hidden, "tensor", axis=1, tiled=True),
-        lax.all_gather(reference_hidden, "tensor", axis=1, tiled=True),
+        push_rounds(reference_hidden, "tensor"),
     )
     logits_t = jnp.dot(
         normalize_full(lax.all_gather(wide_t, "dp", axis=0, tiled=True), target_gain),

time: 409 us -> 409 us (level)
  blocking collectives: 193 us -> 174 us
  waiting for transfers between devices: 170 us -> 188 us
    all_gather x1 -> x0, blocking collectives: 42.1 us -> none  [local(): lax.all_gather(reference_hidden, 'tensor', axis=1, tiled=True)]
    all_to_all x0 -> x1, blocking collectives: none -> 23.4 us  [push_rounds(): lax.all_to_all(val2, split_axis=0, concat_axis=0, axis_name=device_axis)]
    all_gather x1, waiting for transfers between devices: 39.4 us -> 56.7 us  [local(): lax.all_gather(target_hidden, 'tensor', axis=1, tiled=True)]
where the time goes in v1:
time: 409 us
  waiting for transfers between devices  188 us (46%)
  blocking collectives  174 us (43%)
  matrix products  17.4 us (4%)
  between operations  13.1 us (3%)
  other arithmetic  12.9 us (3%)
    all_gather x1, waiting for transfers between devices, local(): lax.all_gather(wide_t, 'dp', axis=0, tiled=True)  89.3 us
    pmax x1, blocking collectives, local(): peak_t, peak_r = lax.pmax((local_peak_t, local_peak_r), ('dp', 'tensor'))  77 us
    psum x1, blocking collectives, local(): lax.psum((local_total_t, local_total_r), ('dp', 'tensor'))  73.6 us
    all_gather x1, waiting for transfers between devices, local(): lax.all_gather(target_hidden, 'tensor', axis=1, tiled=True)  56.7 us
    all_gather x1, waiting for transfers between devices, local(): lax.all_gather(wide_r, 'dp', axis=0, tiled=True)  41 us
    all_to_all x1, blocking collectives, push_rounds(): lax.all_to_all(val2, split_axis=0, concat_axis=0, axis_name=device_axis)  23.4 us
    dot_general x1, matrix products, local(): jnp.dot(normalize_full(lax.all_gather(wide_t, 'dp', axis=0, tiled=True),...  13.6 us
    reduce_sum x2, other arithmetic, normalize_full(): square_mean = jnp.mean(values * values, axis=1, keepdims=True)  10.3 us
  transfers between devices with their start and end apart: 3, of which 3 were waited for; matrix products, arithmetic and copies ran while one was open for 2% of the time, Pallas kernels for 0%

profile of v1, /device:TPU:1, one launch (start us, length us, event | category | flops | bytes accessed | tf_op | source)
XLA Modules:
  0.0 408.7 jit_solution(14501623712414318337)
XLA Ops:
  6.5 0.0 copy-start
  6.5 0.0 all-gather.4.cloned.1.call-start
  6.5 0.7 all-gather.4.cloned.1.call-update
  7.3 0.0 all-gather.8.cloned.1.call-start
  7.3 0.7 stack.2
  8.0 23.4 %all_to_all.5 = bf16[16,32,256]{2,1,0:T(8,128)(2,1)S(1)} all-to-all(bf16[16,32,256]{2,1,0:T(8,128)(2,1)S(1)} %stack.2), channel_id=1, replica_groups=mesh['dp'=16,'tensor'=16] {'tensor'}, dimensions={0} | all-to-all | bytes 524288 | tf_op jit(solution)/shard_map/all_to_all | solution.py:13
  31.4 0.7 copy.11
  32.1 0.0 all-gather.8.cloned.1.call-update
  32.2 0.0 all-gather.6.cloned.1.call-start
  32.2 56.7 %all-gather.4.cloned.1.call-done = bf16[32,16384]{1,0:T(8,128)(2,1)} async-done(((bf16[32,1024]{1,0:T(8,128)(2,1)}), bf16[32,16384]{1,0:T(8,128)(2,1)}) %all-gather.4.cloned.1.call-update) | async-done | bytes 1048592 | tf_op jit(solution)/shard_map/all_gather | solution.py:27
  88.9 0.0 all-gather.6.cloned.1.call-update
  88.9 0.7 convert_element_type.22
  89.6 0.8 convert_element_type.19
  90.4 41.0 %all-gather.8.cloned.1.call-done = bf16[512,4096]{1,0:T(8,128)(2,1)} async-done(((bf16[32,4096]{1,0:T(8,128)(2,1)}), bf16[512,4096]{1,0:T(8,128)(2,1)}) %all-gather.8.cloned.1.call-update) | async-done | bytes 4194320 | tf_op jit(solution)/shard_map/all_gather | solution.py:36
  131.4 3.1 fusion.7
  134.5 0.0 copy-done
  134.5 3.8 fusion.14
  138.3 89.3 %all-gather.6.cloned.1.call-done = bf16[512,16384]{1,0:T(8,128)(2,1)} async-done(((bf16[32,16384]{1,0:T(8,128)(2,1)}), bf16[512,16384]{1,0:T(8,128)(2,1)}) %all-gather.6.cloned.1.call-update) | async-done | bytes 16777232 | tf_op jit(solution)/shard_map/all_gather | solution.py:31
  227.5 7.2 %fusion = f32[512]{0:T(512)S(1)} fusion(bf16[512,16384]{1,0:T(8,128)(2,1)} %all-gather.6.cloned.1.call-done), kind=kLoop, calls=%fused_computation.2 | loop fusion | flops 25165312 | bytes 16779264 | tf_op jit(solution)/shard_map/reduce_sum | solution.py:19
  234.8 13.6 %fusion.15 = (f32[512]{0:T(512)S(1)}, f32[512,256]{0,1:T(8,128)S(1)}) fusion(bf16[16384,256]{1,0:T(8,128)(2,1)} %param.8, bf16[512,16384]{1,0:T(8,128)(2,1)} %all-gather.6.cloned.1.call-done, f32[16384]{0:T(1024)S(1)} %convert_element_type.19, f32[512]{0:T(512)S(1)} %add_rsqrt_fusion.1), kind=kOutput, calls=%fused_computation.24 | convolution fusion | flops 4328652288 | bytes 25759744 | tf_op jit(solution)/shard_map/dot_general | solution.py:30
  248.4 77.0 %all-reduce.1 = (f32[512]{0:T(512)S(1)}, f32[512]{0:T(512)S(1)}) all-reduce(f32[512]{0:T(512)S(1)} %get-tuple-element.9, f32[512]{0:T(512)S(1)} %get-tuple-element.11), channel_id=1, replica_groups=mesh['dp'=16,'tensor'=16] {'dp','tensor'}, use_global_device_ids=true, to_apply=%region_7.0 | all-reduce | flops 1024 | bytes 8192 | tf_op jit(solution)/shard_map/pmax | solution.py:42
  325.4 0.2 exponential_reduce_fusion
  325.6 73.6 %all-reduce = (f32[512]{0:T(512)S(1)}, f32[512]{0:T(512)S(1)}) all-reduce(f32[512]{0:T(512)S(1)} %get-tuple-element.13, f32[512]{0:T(512)S(1)} %get-tuple-element.14), channel_id=1, replica_groups=mesh['dp'=16,'tensor'=16] {'dp','tensor'}, use_global_device_ids=true, to_apply=%region_9.0 | all-reduce | flops 1024 | bytes 8192 | tf_op jit(solution)/shard_map/psum | solution.py:45
  399.2 0.9 minimum_add_fusion
  400.1 2.0 copy.10
  (4 shorter events, 0.0 us)
Async XLA Ops:
  6.5 128.0 %copy-start = (bf16[4096,256]{1,0:T(8,128)(2,1)S(1)}, bf16[4096,256]{1,0:T(8,128)(2,1)}, u32[]{:S(2)}) copy-start(bf16[4096,256]{1,0:T(8,128)(2,1)} %param.11) | copy-start | bytes 6291460
  6.5 82.4 %all-gather.4.cloned.1.call-start = ((), (), s32[]{:S(2)}) async-start(), calls=%async_computation.1 | async-start | bytes 1114112 | tf_op jit(solution)/shard_map/all_gather | solution.py:27
  7.3 124.1 %all-gather.8.cloned.1.call-start = ((), (), s32[]{:S(2)}) async-start(), calls=%async_computation.3 | async-start | bytes 4456448 | tf_op jit(solution)/shard_map/all_gather | solution.py:36
  32.2 195.4 %all-gather.6.cloned.1.call-start = ((), (), s32[]{:S(2)}) async-start(), calls=%async_computation.2 | async-start | bytes 17825792 | tf_op jit(solution)/shard_map/all_gather | solution.py:31
Sparse Core Ops, SparseCore 0:
  10.0 78.9 all-gather.3
  90.8 40.6 all-gather.7
  133.3 94.2 all-gather.5
